TPU v7x, 32 devices: a whole 2x2x4 slice. The times are simulated.
32 devices in a mesh: expert: 8 (over z, core), dp: 4 (over y, x).
Axes of the slice: x: 2, y: 2, z: 4, core: 2. Of those that a mesh axis runs over, the one named last changes fastest.
Arguments:
- tokens: bfloat16 [4096, 1024], P(('expert', 'dp')), may hold values from -6 to 6
- out_grad: bfloat16 [4096, 1024], P(('expert', 'dp')), may hold values from -0.59765625 to 0.59765625
- expert_ids: int32 [4096, 3], P(('expert', 'dp')), may hold values from 0 to 7, all different within a row; in each aligned block of 128 rows (0 to 127, 128 to 255, ...) at most 64 rows name the same one
- gate_probs: float32 [4096, 3], P(('expert', 'dp')), may hold values from 0.05 to 0.5
- w_gate: bfloat16 [8, 1024, 384], P('expert'), may hold values from -0.1875 to 0.1875
- w_up: bfloat16 [8, 1024, 384], P('expert'), may hold values from -0.1875 to 0.1875
- w_down: bfloat16 [8, 384, 1024], P('expert'), may hold values from -0.3125 to 0.3125
Outputs:
- grad_gate: bfloat16 [8, 1024, 384], P('expert', 'dp')
- grad_up: bfloat16 [8, 1024, 384], P('expert', 'dp')
- grad_down: bfloat16 [8, 384, 1024], P('expert', 'dp')
Inputs may be any that keep to these rules, and one draw needn't show every extreme that they name: `expert_ids`: each row names 3 different experts. In the 128 rows of one device no expert is named by more than 64 rows, a bound that some block reaches.
All inputs are finite; a program needn't handle non-finite values.
Results may differ from a plain program's by a relative error of at most 0.018.
Values may be sent and summed in bfloat16 or wider, within the bound.
A program may use at most 64 MiB of HBM per device.

v0:
```python
import jax
import jax.numpy as jnp
from jax import lax
from jax.sharding import PartitionSpec as P


def contract_rows(left, right):
    return lax.dot_general(
        left, right, (((0,), (0,)), ((), ())), preferred_element_type=jnp.float32
    )


def shards(tokens, out_grad, expert_ids, gate_probs, w_gate, w_up, w_down):
    experts = lax.axis_size("expert")
    tok_rows = tokens.shape[0]
    top_k = expert_ids.shape[1]
    width = tokens.shape[1]
    capacity = min(tok_rows, 4 * tok_rows * top_k // (3 * experts))
    columns = jnp.arange(experts, dtype=jnp.int32)
    hits = (expert_ids[:, :, None] == columns).astype(jnp.int32)
    token_hits = jnp.sum(hits, axis=1)
    before = jnp.cumsum(token_hits, axis=0) - token_hits
    rank = jnp.sum(hits * before[:, None, :], axis=2)
    scaled = (gate_probs[:, :, None] * out_grad[:, None, :].astype(jnp.float32)).astype(
        jnp.bfloat16
    )
    repeated = jnp.broadcast_to(tokens[:, None, :], scaled.shape)
    flat_slot = (expert_ids * capacity + rank).reshape(-1)
    send_in = (
        jnp.zeros((experts * capacity, width), jnp.bfloat16)
        .at[flat_slot]
        .set(repeated.reshape(-1, width))
    )
    send_grad = (
        jnp.zeros((experts * capacity, width), jnp.bfloat16)
        .at[flat_slot]
        .set(scaled.reshape(-1, width))
    )
    send_in = send_in.reshape(experts, capacity, width)
    send_grad = send_grad.reshape(experts, capacity, width)
    got_in, got_grad = (
        lax.all_to_all(send_in, "expert", split_axis=0, concat_axis=0, tiled=True),
        lax.all_to_all(send_grad, "expert", split_axis=0, concat_axis=0, tiled=True),
    )
    rows_in = got_in.reshape(-1, width)
    rows_grad = got_grad.reshape(-1, width)
    gate_pre = jnp.dot(rows_in, w_gate[0], preferred_element_type=jnp.float32)
    up_pre = jnp.dot(rows_in, w_up[0], preferred_element_type=jnp.float32)
    sigma = jax.nn.sigmoid(gate_pre)
    active = gate_pre * sigma
    hidden = (active * up_pre).astype(jnp.bfloat16)
    grad_down = contract_rows(hidden, rows_grad)
    grad_hidden = lax.dot_general(
        rows_grad, w_down[0], (((1,), (1,)), ((), ())), preferred_element_type=jnp.float32
    )
    grad_upper = (grad_hidden * active).astype(jnp.bfloat16)
    grad_gate_pre = (grad_hidden * up_pre * sigma * (1.0 + gate_pre * (1.0 - sigma))).astype(
        jnp.bfloat16
    )
    grad_gate = contract_rows(rows_in, grad_gate_pre)
    grad_up = contract_rows(rows_in, grad_upper)
    sum_gate, sum_up, sum_down = (
        lax.psum_scatter(
            grad_gate[None].astype(jnp.bfloat16), "dp", scatter_dimension=1, tiled=True
        ).astype(jnp.float32),
        lax.psum_scatter(
            grad_up[None].astype(jnp.bfloat16), "dp", scatter_dimension=1, tiled=True
        ).astype(jnp.float32),
        lax.psum_scatter(
            grad_down[None].astype(jnp.bfloat16), "dp", scatter_dimension=1, tiled=True
        ).astype(jnp.float32),
    )
    return (
        sum_gate.astype(jnp.bfloat16),
        sum_up.astype(jnp.bfloat16),
        sum_down.astype(jnp.bfloat16),
    )


def solution(mesh):
    return jax.shard_map(
        shards,
        mesh=mesh,
        in_specs=(
            P(("expert", "dp"), None),
            P(("expert", "dp"), None),
            P(("expert", "dp"), None),
            P(("expert", "dp"), None),
            P("expert", None, None),
            P("expert", None, None),
            P("expert", None, None),
        ),
        out_specs=(P("expert", "dp", None), P("expert", "dp", None), P("expert", "dp", None)),
        check_vma=False,
    )
```

profile of v0, /device:TPU:0, one launch (start us, length us, event | category | flops | bytes accessed | tf_op | source)
XLA Modules:
  0.0 173.8 jit_solution(15862193931348732459)
XLA Ops:
  7.2 0.8 convert_reduce_fusion
  8.3 0.7 select_reduce_fusion
  9.0 0.7 multiply_add_fusion
  10.0 1.3 broadcast_in_dim.2
  11.3 0.7 reshape.83
  12.0 3.1 %scatter_custom_fusion = bf16[512,1024]{1,0:T(8,128)(2,1)} fusion(s32[384]{0:T(512)S(1)} %fusion.18, bf16[384,1024]{1,0:T(8,128)(2,1)S(1)} %reshape.83, bf16[]{:T(256)} %constant.5.clone.1), kind=kCustom, calls=%fused_computation.23 | custom fusion | bytes 1048578 | tf_op jit(solution)/shard_map/scatter | solution.py:32
  15.1 6.4 %all-to-all-start = ((bf16[8,64,1024]{2,1,0:T(8,128)(2,1)}), bf16[8,64,1024]{2,1,0:T(8,128)(2,1)S(1)}, u32[]{:S(2)}, u32[]{:S(2)}) async-start(bf16[8,64,1024]{2,1,0:T(8,128)(2,1)} %bitcast), calls=%async_computation | async-start | bytes 2097152 | tf_op jit(solution)/shard_map/all_to_all | solution.py:42
  21.5 1.9 %mul.59 = f32[128,3,1024]{2,1,0:T(4,128)} broadcast(bf16[128,1024]{1,0:T(8,128)(2,1)S(1)} %copy-done.5), dimensions={0,2} | broadcast | bytes 1835008 | tf_op jit(solution)/shard_map/mul | solution.py:24
  23.4 2.7 %mul.60 = f32[384,1024]{1,0:T(8,128)S(1)} reshape(f32[128,3,1024]{2,1,0:T(4,128)} %mul.59) | data formatting | bytes 3145728 | tf_op jit(solution)/shard_map/mul | solution.py:24
  26.2 0.2 mul.57
  26.5 3.1 %scatter_custom_fusion.1 = bf16[512,1024]{1,0:T(8,128)(2,1)} fusion(s32[384]{0:T(512)S(1)} %fusion.18, f32[384,1024]{1,0:T(8,128)S(1)} %mul.60, f32[384]{0:T(512)S(1)} %mul.57, bf16[]{:T(256)} %constant.5.clone.1), kind=kCustom, calls=%fused_computation.9 | custom fusion | flops 786432 | bytes 2623490 | tf_op jit(solution)/shard_map/scatter | solution.py:37
  29.6 18.4 %all-to-all-done = bf16[8,64,1024]{2,1,0:T(8,128)(2,1)S(1)} async-done(((bf16[8,64,1024]{2,1,0:T(8,128)(2,1)}), bf16[8,64,1024]{2,1,0:T(8,128)(2,1)S(1)}, u32[]{:S(2)}, u32[]{:S(2)}) %all-to-all-start) | async-done | bytes 1048608 | tf_op jit(solution)/shard_map/all_to_all | solution.py:42
  48.0 3.6 %all-to-all-start.1 = ((bf16[8,64,1024]{2,1,0:T(8,128)(2,1)}), bf16[8,64,1024]{2,1,0:T(8,128)(2,1)S(1)}, u32[]{:S(2)}, u32[]{:S(2)}) async-start(bf16[8,64,1024]{2,1,0:T(8,128)(2,1)} %bitcast.31), calls=%async_computation.1 | async-start | bytes 2097152 | tf_op jit(solution)/shard_map/all_to_all | solution.py:43
  51.7 1.6 fusion.4
  53.3 1.6 fusion.6
  54.9 23.2 %all-to-all-done.1 = bf16[8,64,1024]{2,1,0:T(8,128)(2,1)S(1)} async-done(((bf16[8,64,1024]{2,1,0:T(8,128)(2,1)}), bf16[8,64,1024]{2,1,0:T(8,128)(2,1)S(1)}, u32[]{:S(2)}, u32[]{:S(2)}) %all-to-all-start.1) | async-done | bytes 1048608 | tf_op jit(solution)/shard_map/all_to_all | solution.py:43
  78.1 2.0 %fusion.8 = f32[512,384]{1,0:T(8,128)S(1)} fusion(bf16[512,1024]{1,0:T(8,128)(2,1)S(1)} %bitcast.29, bf16[1,384,1024]{2,1,0:T(8,128)(2,1)} %param.13), kind=kOutput, calls=%fused_computation.14 | convolution fusion | flops 402653184 | bytes 2621440 | tf_op jit(solution)/shard_map/dot_general | solution.py:53
  80.1 0.9 copy-done.4
  81.0 1.8 %fusion = bf16[1,1024,384]{2,1,0:T(8,128)(2,1)} fusion(bf16[512,1024]{1,0:T(8,128)(2,1)S(1)} %bitcast.27, f32[512,384]{1,0:T(8,128)S(1)} %copy-done.2, f32[512,384]{1,0:T(8,128)S(1)} %fusion.8, f32[512,384]{1,0:T(8,128)S(1)} %copy-done.3), kind=kOutput, calls=%fused_computation.6 | convolution fusion | flops 405012480 | bytes 4194304 | tf_op jit(solution)/shard_map/dot_general | solution.py:8
  82.8 3.1 %fusion.1 = bf16[1,1024,384]{2,1,0:T(8,128)(2,1)} fusion(bf16[512,1024]{1,0:T(8,128)(2,1)S(1)} %bitcast.28, f32[512,384]{1,0:T(8,128)} %copy-done.4, f32[512,384]{1,0:T(8,128)} %fusion.4), kind=kOutput, calls=%fused_computation.7 | convolution fusion | flops 404226048 | bytes 3407872 | tf_op jit(solution)/shard_map/dot_general | solution.py:8
  86.0 2.9 %fusion.2 = bf16[1,384,1024]{2,1,0:T(8,128)(2,1)} fusion(bf16[512,1024]{1,0:T(8,128)(2,1)S(1)} %bitcast.30, f32[512,384]{1,0:T(8,128)} %fusion.6, f32[512,384]{1,0:T(8,128)} %fusion.4), kind=kOutput, calls=%fused_computation.8 | convolution fusion | flops 404226048 | bytes 3407872 | tf_op jit(solution)/shard_map/dot_general | solution.py:8
  88.9 19.1 %reduce-scatter.4.cloned.1.call-done = bf16[1,256,384]{2,1,0:T(8,128)(2,1)} async-done(((bf16[1,1024,384]{2,1,0:T(8,128)(2,1)}), bf16[1,256,384]{2,1,0:T(8,128)(2,1)}) %reduce-scatter.4.cloned.1.call-update) | async-done | bytes 196624 | tf_op jit(solution)/shard_map/reduce_scatter | solution.py:63
  108.0 29.7 %reduce-scatter.6.cloned.1.call-done = bf16[1,256,384]{2,1,0:T(8,128)(2,1)} async-done(((bf16[1,1024,384]{2,1,0:T(8,128)(2,1)}), bf16[1,256,384]{2,1,0:T(8,128)(2,1)}) %reduce-scatter.6.cloned.1.call-update) | async-done | bytes 196624 | tf_op jit(solution)/shard_map/reduce_scatter | solution.py:66
  137.6 29.7 %reduce-scatter.8.cloned.1.call-done = bf16[1,96,1024]{2,1,0:T(8,128)(2,1)} async-done(((bf16[1,384,1024]{2,1,0:T(8,128)(2,1)}), bf16[1,96,1024]{2,1,0:T(8,128)(2,1)}) %reduce-scatter.8.cloned.1.call-update) | async-done | bytes 196624 | tf_op jit(solution)/shard_map/reduce_scatter | solution.py:69
  (27 shorter events, 1.0 us)
Async XLA Ops:
  7.2 44.5 %copy-start = (bf16[1,1024,384]{2,1,0:T(8,128)(2,1)S(1)}, bf16[1,1024,384]{2,1,0:T(8,128)(2,1)}, u32[]{:S(2)}) copy-start(bf16[1,1024,384]{2,1,0:T(8,128)(2,1)} %param.11) | copy-start | bytes 2359300
  12.0 9.5 %copy-start.5 = (bf16[128,1024]{1,0:T(8,128)(2,1)S(1)}, bf16[128,1024]{1,0:T(8,128)(2,1)}, u32[]{:S(2)}) copy-start(bf16[128,1024]{1,0:T(8,128)(2,1)} %param.8) | copy-start | bytes 786436
  15.1 32.9 %all-to-all-start = ((bf16[8,64,1024]{2,1,0:T(8,128)(2,1)}), bf16[8,64,1024]{2,1,0:T(8,128)(2,1)S(1)}, u32[]{:S(2)}, u32[]{:S(2)}) async-start(bf16[8,64,1024]{2,1,0:T(8,128)(2,1)} %bitcast), calls=%async_computation | async-start | bytes 2097152 | tf_op jit(solution)/shard_map/all_to_all | solution.py:42
  23.4 2.7 %copy-start.6 = (f32[128,3]{0,1:T(4,128)S(1)}, f32[128,3]{0,1:T(4,128)}, u32[]{:S(2)}) copy-start(f32[128,3]{0,1:T(4,128)} %param.10) | copy-start | bytes 4612
  48.0 30.1 %all-to-all-start.1 = ((bf16[8,64,1024]{2,1,0:T(8,128)(2,1)}), bf16[8,64,1024]{2,1,0:T(8,128)(2,1)S(1)}, u32[]{:S(2)}, u32[]{:S(2)}) async-start(bf16[8,64,1024]{2,1,0:T(8,128)(2,1)} %bitcast.31), calls=%async_computation.1 | async-start | bytes 2097152 | tf_op jit(solution)/shard_map/all_to_all | solution.py:43
  51.6 56.4 %reduce-scatter.4.cloned.1.call-start = ((), (), s32[]{:S(2)}) async-start(), calls=%async_computation.5 | async-start | bytes 983040 | tf_op jit(solution)/shard_map/reduce_scatter | solution.py:63
  51.7 1.6 copy-start.1
  78.1 2.9 %copy-start.2 = (f32[512,384]{1,0:T(8,128)S(1)}, f32[512,384]{1,0:T(8,128)}, u32[]{:S(2)}) copy-start(f32[512,384]{1,0:T(8,128)} %fusion.4) | copy-start | bytes 2359300
  78.1 2.9 %copy-start.3 = (f32[512,384]{1,0:T(8,128)S(1)}, f32[512,384]{1,0:T(8,128)}, u32[]{:S(2)}) copy-start(f32[512,384]{1,0:T(8,128)} %fusion.6) | copy-start | bytes 2359300
  80.1 0.9 copy-start.4
  82.8 54.9 %reduce-scatter.6.cloned.1.call-start = ((), (), s32[]{:S(2)}) async-start(), calls=%async_computation.6 | async-start | bytes 983040 | tf_op jit(solution)/shard_map/reduce_scatter | solution.py:66
  85.9 81.4 %reduce-scatter.8.cloned.1.call-start = ((), (), s32[]{:S(2)}) async-start(), calls=%async_computation.7 | async-start | bytes 983040 | tf_op jit(solution)/shard_map/reduce_scatter | solution.py:69
Sparse Core Ops, SparseCore 0:
  82.9 25.0 reduce-scatter.3
  111.5 26.1 reduce-scatter.5
  141.1 26.1 reduce-scatter.7
where the time goes:
time: 174 us
  waiting for transfers between devices  120 us (69%)
  between operations  13.8 us (8%)
  matrix products  12.9 us (7%)
  local copies, waits for them, and re-layouts  11.4 us (7%)
  starting transfers between devices  10 us (6%)
  other arithmetic  5.52 us (3%)
    reduce_scatter x1, waiting for transfers between devices, shards(): lax.psum_scatter(grad_down[None].astype(jnp.bfloat16), 'dp', scatter_dime...  29.7 us
    reduce_scatter x1, waiting for transfers between devices, shards(): lax.psum_scatter(grad_up[None].astype(jnp.bfloat16), 'dp', scatter_dimens...  29.7 us
    all_to_all x1, waiting for transfers between devices, shards(): lax.all_to_all(send_grad, 'expert', split_axis=0, concat_axis=0, tiled=True)  23.2 us
    reduce_scatter x1, waiting for transfers between devices, shards(): lax.psum_scatter(grad_gate[None].astype(jnp.bfloat16), 'dp', scatter_dime...  19.1 us
    all_to_all x1, waiting for transfers between devices, shards(): lax.all_to_all(send_in, 'expert', split_axis=0, concat_axis=0, tiled=True)  18.4 us
    dot_general x3, matrix products, contract_rows(): lax.dot_general(left, right, (((0,), (0,)), ((), ())), preferred_element_...  7.74 us
    all_to_all x1, starting transfers between devices, shards(): lax.all_to_all(send_in, 'expert', split_axis=0, concat_axis=0, tiled=True)  6.35 us
    mul x3, local copies, waits for them, and re-layouts, shards(): gate_probs[:, :, None] * out_grad[:, None, :].astype(jnp.float32)  4.83 us
  transfers between devices with their start and end apart: 5, of which 5 were waited for; matrix products, arithmetic and copies ran while one was open for 10% of the time, Pallas kernels for 0%

commit v1 on v0

v1 whole, which is shorter than its diff:
```python
import functools

import jax
import jax.numpy as jnp
from jax import lax
from jax.experimental import pallas as pl
from jax.experimental.pallas import tpu as pltpu
from jax.sharding import PartitionSpec as P

MESH = pl.DeviceIdType.MESH
CORES = 2


def kernel(
    n_e, n_d,
    tok, cot, ids, probs, wg_in, wu_in, wd_in,
    out_g, out_u, out_d,
    X, G, PT, WG, WU, WD, XT, HT, GG, S, SB, SD, RB, RD, ACC, ACD,
    lsem, chain_s, sib_s, blk_r, rs_s, rs_r,
):
    rows, width = tok.shape
    hid = wg_in.shape[2]
    top = ids.shape[0]
    n_z = n_e // CORES
    me = lax.axis_index("expert")
    dd = lax.axis_index("dp")
    z, c = me // CORES, me % CORES
    sib = z * CORES + (1 - c)

    erow = lax.broadcasted_iota(jnp.int32, PT.shape[1:], 0)
    table = jnp.zeros(PT.shape[1:], jnp.float32)
    for k in range(top):
        table = table + jnp.where(ids[k : k + 1, :] == erow, probs[k : k + 1, :], 0.0)
    PT[me] = table

    barrier = pltpu.get_barrier_semaphore()
    for step in (-1, 1):
        @pl.when(jnp.logical_and(z + step >= 0, z + step < n_z))
        def _():
            pl.semaphore_signal(barrier, inc=1, device_id={"expert": me + step * CORES}, device_id_type=MESH)
    pl.semaphore_signal(barrier, inc=1, device_id={"expert": sib}, device_id_type=MESH)
    for i in range(1, n_d):
        pl.semaphore_signal(barrier, inc=1, device_id={"dp": (dd + i) % n_d}, device_id_type=MESH)
    arrivals = n_d + jnp.where(z > 0, 1, 0) + jnp.where(z < n_z - 1, 1, 0)
    pl.semaphore_wait(barrier, arrivals)

    full = (PT, X, G)
    own = (PT.at[me], tok, cot)

    def hop(k, d, src, mine):
        there = me + (CORES if d == 0 else -CORES)
        return pltpu.make_async_remote_copy(
            src_ref=own[k] if mine else full[k].at[src],
            dst_ref=full[k].at[src],
            send_sem=chain_s.at[k, d, src],
            recv_sem=blk_r.at[k, src],
            device_id={"expert": there},
            device_id_type=MESH,
        )

    def across(k, src, mine):
        return pltpu.make_async_remote_copy(
            src_ref=own[k] if mine else full[k].at[src],
            dst_ref=full[k].at[src],
            send_sem=sib_s.at[k, src],
            recv_sem=blk_r.at[k, src],
            device_id={"expert": sib},
            device_id_type=MESH,
        )

    def can(d):
        return z < n_z - 1 if d == 0 else z > 0

    for k in range(3):
        for d in range(2):
            @pl.when(can(d))
            def _():
                hop(k, d, me, True).start()
        across(k, me, True).start()
    local = [
        pltpu.make_async_copy(tok, X.at[me], lsem.at[0]),
        pltpu.make_async_copy(cot, G.at[me], lsem.at[1]),
        pltpu.make_async_copy(wg_in.at[0], WG, lsem.at[2]),
        pltpu.make_async_copy(wu_in.at[0], WU, lsem.at[3]),
        pltpu.make_async_copy(wd_in.at[0], WD, lsem.at[4]),
    ]
    for copy in local:
        copy.start()
    for copy in local:
        copy.wait()

    pair = CORES * rows

    def forward(zz):
        for k in range(3):
            across(k, zz * CORES + (1 - c), False).wait_recv()
        at = pl.multiple_of(zz * pair, pair)
        x = X[pl.ds(zz * CORES, CORES)].reshape(pair, width)
        XT[:, pl.ds(at, pair)] = x.T
        parts = []
        for h in range(CORES):
            p = PT[zz * CORES + h, pl.ds(me, 1), :]
            p = jnp.broadcast_to(p, (rows, rows)).T[:, :1]
            parts.append((p * G[zz * CORES + h].astype(jnp.float32)).astype(jnp.bfloat16))
        scaled = jnp.concatenate(parts, axis=0)
        S[pl.ds(at, pair), :] = scaled
        gate = jnp.dot(x, WG[...], preferred_element_type=jnp.float32)
        up = jnp.dot(x, WU[...], preferred_element_type=jnp.float32)
        gh = lax.dot_general(scaled, WD[...], (((1,), (1,)), ((), ())), preferred_element_type=jnp.float32)
        sigma = jax.nn.sigmoid(gate)
        active = gate * sigma
        HT[:, pl.ds(at, pair)] = (active * up).astype(jnp.bfloat16).T
        GG[pl.ds(at, pair), hid:] = (gh * active).astype(jnp.bfloat16)
        GG[pl.ds(at, pair), :hid] = (gh * up * sigma * (1.0 + gate * (1.0 - sigma))).astype(jnp.bfloat16)

    @pl.loop(0, n_z)
    def _(s):
        @pl.loop(0, 2)
        def _(d):
            zz = jnp.where(d == 0, z - s, z + s)

            @pl.when((zz >= 0) & (zz < n_z) & ((s > 0) | (d == 0)))
            def _():
                forward(zz)

        for k in range(3):
            for d in range(2):
                zz = z - (s + 1) if d == 0 else z + (s + 1)
                src = zz * CORES + c

                @pl.when((zz >= 0) & (zz < n_z))
                def _():
                    hop(k, d, src, False).wait_recv()

                    @pl.when(can(d))
                    def _():
                        hop(k, d, src, False).start()

                    across(k, src, False).start()

    piece, hpiece = width // n_d, hid // n_d
    chunk = max(piece, min(256, width))
    n_c = width // chunk
    hchunk, per = hid // n_c, chunk // piece

    def give(k, j, slot):
        src = SB.at[pl.ds(pl.multiple_of(j * piece, piece), piece)] if k == 0 else SD.at[j]
        dst = RB.at[slot] if k == 0 else RD.at[slot]
        return pltpu.make_async_remote_copy(
            src_ref=src, dst_ref=dst, send_sem=rs_s.at[k, j], recv_sem=rs_r.at[k, slot],
            device_id={"dp": j}, device_id_type=MESH,
        )

    @pl.loop(0, n_c)
    def _(i):
        cc = (dd // per + 1 + i) % n_c
        at = pl.multiple_of(cc * chunk, chunk)
        hat = pl.multiple_of(cc * hchunk, hchunk)
        SB[pl.ds(at, chunk), :] = jnp.dot(
            XT[pl.ds(at, chunk), :], GG[...], preferred_element_type=jnp.float32
        ).astype(jnp.bfloat16)
        down = jnp.dot(HT[pl.ds(hat, hchunk), :], S[...], preferred_element_type=jnp.float32).astype(jnp.bfloat16)
        for q in range(per):
            SD[cc * per + q] = down[q * hpiece : (q + 1) * hpiece]
        for q in range(per):
            j = cc * per + q

            @pl.when(j != dd)
            def _():
                give(0, j, dd).start()
                give(1, j, dd).start()

    ACC[...] = SB[pl.ds(pl.multiple_of(dd * piece, piece), piece), :].astype(jnp.float32)
    ACD[...] = SD[dd].astype(jnp.float32)

    @pl.loop(1, n_d)
    def _(i):
        j = (dd + n_d - i) % n_d
        give(0, (dd + 1) % n_d, j).wait_recv()
        ACC[...] += RB[j].astype(jnp.float32)
        give(1, (dd + 1) % n_d, j).wait_recv()
        ACD[...] += RD[j].astype(jnp.float32)

    out_g[0] = ACC[:, :hid].astype(jnp.bfloat16)
    out_u[0] = ACC[:, hid:].astype(jnp.bfloat16)
    out_d[0] = ACD[...].astype(jnp.bfloat16)

    @pl.loop(1, n_d)
    def _(i):
        j = (dd + i) % n_d
        give(0, j, dd).wait_send()
        give(1, j, dd).wait_send()

    @pl.loop(0, n_z)
    def _(s):
        for k in range(3):
            for d in range(2):
                zz = z - s if d == 0 else z + s
                src = zz * CORES + c

                @pl.when((zz >= 0) & (zz < n_z) & can(d))
                def _():
                    hop(k, d, src, False).wait_send()

            across(k, s * CORES + c, False).wait_send()


def solution(mesh):
    n_e, n_d = mesh.shape["expert"], mesh.shape["dp"]

    def step(tokens, out_grad, expert_ids, gate_probs, w_gate, w_up, w_down):
        rows, width = tokens.shape
        hid = w_gate.shape[2]
        total = n_e * rows
        lanes = -(-n_e // 8) * 8
        bf, f32 = jnp.bfloat16, jnp.float32
        vmem = pl.BlockSpec(memory_space=pltpu.VMEM)
        hbm = pl.BlockSpec(memory_space=pl.ANY)
        piece, hpiece = width // n_d, hid // n_d
        dma = pltpu.SemaphoreType.DMA
        return pl.pallas_call(
            functools.partial(kernel, n_e, n_d),
            out_shape=(
                jax.ShapeDtypeStruct((1, piece, hid), bf),
                jax.ShapeDtypeStruct((1, piece, hid), bf),
                jax.ShapeDtypeStruct((1, hpiece, width), bf),
            ),
            in_specs=[hbm, hbm, vmem, vmem, hbm, hbm, hbm],
            out_specs=(vmem, vmem, vmem),
            scratch_shapes=[
                pltpu.VMEM((n_e, rows, width), bf),
                pltpu.VMEM((n_e, rows, width), bf),
                pltpu.VMEM((n_e, lanes, rows), f32),
                pltpu.VMEM((width, hid), bf),
                pltpu.VMEM((width, hid), bf),
                pltpu.VMEM((hid, width), bf),
                pltpu.VMEM((width, total), bf),
                pltpu.VMEM((hid, total), bf),
                pltpu.VMEM((total, 2 * hid), bf),
                pltpu.VMEM((total, width), bf),
                pltpu.VMEM((width, 2 * hid), bf),
                pltpu.VMEM((n_d, hpiece, width), bf),
                pltpu.VMEM((n_d, piece, 2 * hid), bf),
                pltpu.VMEM((n_d, hpiece, width), bf),
                pltpu.VMEM((piece, 2 * hid), f32),
                pltpu.VMEM((hpiece, width), f32),
                dma((5,)),
                dma((3, 2, n_e)),
                dma((3, n_e)),
                dma((3, n_e)),
                dma((2, n_d)),
                dma((2, n_d)),
            ],
            compiler_params=pltpu.CompilerParams(
                collective_id=0, has_side_effects=True, vmem_limit_bytes=60 * 1024 * 1024
            ),
        )(tokens, out_grad, expert_ids.T, gate_probs.T, w_gate, w_up, w_down)

    spread = P(("expert", "dp"), None)
    return jax.shard_map(
        step,
        mesh=mesh,
        in_specs=(spread, spread, spread, spread) + (P("expert", None, None),) * 3,
        out_specs=(P("expert", "dp", None),) * 3,
        check_vma=False,
    )
```

time: 174 us -> 77.4 us (0.44)
  waiting for transfers between devices: 120 us -> 0 us
  Pallas kernels: 0 us -> 73.2 us
  between operations: 13.8 us -> 0.65 us
  matrix products: 12.9 us -> 0 us
  starting transfers between devices: 10 us -> 0 us
  local copies, waits for them, and re-layouts: 11.4 us -> 3.34 us
  other arithmetic: 5.52 us -> 0 us
    reduce_scatter x3 -> x0, waiting for transfers between devices: 78.4 us -> none  [the longest x1 29.7 us: shards(): lax.psum_scatter(grad_down[None].astype(jnp.bfloat16), 'dp', scatter_dime...]
    pallas_call x0 -> x1, Pallas kernels: none -> 73.2 us  [step(): pl.pallas_call(functools.partial(kernel, n_e, n_d), out_shape=(jax.ShapeD...]
    all_to_all x2 -> x0, waiting for transfers between devices: 41.6 us -> none  [the longest x1 23.2 us: shards(): lax.all_to_all(send_grad, 'expert', split_axis=0, concat_axis=0, tiled=True)]
    dot_general x6 -> x0, matrix products: 12.9 us -> none  [the longest x3 7.74 us: contract_rows(): lax.dot_general(left, right, (((0,), (0,)), ((), ())), preferred_element_...]
    all_to_all x2 -> x0, starting transfers between devices: 9.91 us -> none  [the longest x1 6.35 us: shards(): lax.all_to_all(send_in, 'expert', split_axis=0, concat_axis=0, tiled=True)]
    mul x3 -> x0, local copies, waits for them, and re-layouts: 4.83 us -> none  [shards(): gate_probs[:, :, None] * out_grad[:, None, :].astype(jnp.float32)]
    scatter x1 -> x0, other arithmetic: 3.15 us -> none  [shards(): send_grad = jnp.zeros((experts * capacity, width), jnp.bfloat16).at[flat_...]
    scatter x1 -> x0, local copies, waits for them, and re-layouts: 3.11 us -> none  [shards(): send_in = jnp.zeros((experts * capacity, width), jnp.bfloat16).at[flat_sl...]
  transfers between devices with their start and end apart: 5 -> 0, of which waited for: 5 -> 0; matrix products, arithmetic and copies ran while one was open for 10% -> 0% of each run, Pallas kernels for 0% -> 0%
where the time goes in v1:
time: 77.4 us; the launch traced here: 77.2 us
  Pallas kernels  73.2 us (95%)
  local copies, waits for them, and re-layouts  3.34 us (4%)
    pallas_call x1, Pallas kernels, step(): pl.pallas_call(functools.partial(kernel, n_e, n_d), out_shape=(jax.ShapeD...  73.2 us
    unnamed x7, local copies, waits for them, and re-layouts  3.34 us

profile of v1, /device:TPU:0, one launch (start us, length us, event | category | flops | bytes accessed | tf_op | source)
XLA Modules:
  0.0 77.2 jit_solution(16960894744189728258)
XLA Ops:
  0.6 73.2 %shard_map.94 = (bf16[1,256,384]{2,1,0:T(8,128)(2,1)}, bf16[1,256,384]{2,1,0:T(8,128)(2,1)}, bf16[1,96,1024]{2,1,0:T(8,128)(2,1)}) custom-call(bf16[128,1024]{1,0:T(8,128)(2,1)} %tok.1, bf16[128,1024]{1,0:T(8,128)(2,1)} %cot.1, s32[3,128]{1,0:T(4,128)} %bitcast.2, f32[3,128]{1,0:T(4,128)} %bitcast.3, bf16[1,1024,384]{2,1,0:T(8,128)(2,1)} %wg_in.1, ...), custom_call_target="tpu_custom_call" | custom-call | tf_op jit(solution)/shard_map/pallas_call | solution.py:221
  73.9 0.0 copy-start.1
  73.9 1.7 %copy.13 = bf16[1,256,384]{2,1,0:T(8,128)(2,1)} copy(bf16[1,256,384]{2,1,0:T(8,128)(2,1)} %get-tuple-element.6) | data formatting | bytes 393216
  75.5 0.0 copy-done.1
  75.5 0.0 copy-start
  75.5 0.7 copy.14
  76.2 0.3 copy-done
  76.5 0.7 copy.15
Async XLA Ops:
  73.9 1.7 %copy-start.1 = (bf16[1,256,384]{2,1,0:T(8,128)(2,1)S(1)}, bf16[1,256,384]{2,1,0:T(8,128)(2,1)}, u32[]{:S(2)}) copy-start(bf16[1,256,384]{2,1,0:T(8,128)(2,1)} %get-tuple-element.7) | copy-start | bytes 589828
  75.5 1.0 %copy-start = (bf16[1,96,1024]{2,1,0:T(8,128)(2,1)S(1)}, bf16[1,96,1024]{2,1,0:T(8,128)(2,1)}, u32[]{:S(2)}) copy-start(bf16[1,96,1024]{2,1,0:T(8,128)(2,1)} %get-tuple-element.8) | copy-start | bytes 589828

commit v2 on v1

v2 whole, which is shorter than its diff:
```python
import functools
import math

import jax
import jax.numpy as jnp
from jax import lax
from jax.experimental import pallas as pl
from jax.experimental.pallas import tpu as pltpu
from jax.sharding import PartitionSpec as P

MESH = pl.DeviceIdType.MESH
CORES = 2


def kernel(
    n_e, n_a, n_b,
    tok, cot, ids, probs, wg_in, wu_in, wd_in,
    out_g, out_u, out_d,
    X, G, PT, WG, WU, WD, GU, XT, HT, GG, S, MB, DB, MR, DR, MP, DP, MQ, DQ,
    lsem, chain_s, sib_s, blk_r, one_s, one_r, two_s, two_r,
):
    n_d = n_a * n_b
    rows, width = tok.shape
    hid = wg_in.shape[2]
    top = ids.shape[0]
    n_z = n_e // CORES
    me = lax.axis_index("expert")
    dd = lax.axis_index("dp")
    z, c = me // CORES, me % CORES
    sib = z * CORES + (1 - c)

    erow = lax.broadcasted_iota(jnp.int32, PT.shape[1:], 0)
    table = jnp.zeros(PT.shape[1:], jnp.float32)
    for k in range(top):
        table = table + jnp.where(ids[k : k + 1, :] == erow, probs[k : k + 1, :], 0.0)
    PT[me] = table

    barrier = pltpu.get_barrier_semaphore()
    for step in (-1, 1):
        @pl.when(jnp.logical_and(z + step >= 0, z + step < n_z))
        def _():
            pl.semaphore_signal(barrier, inc=1, device_id={"expert": me + step * CORES}, device_id_type=MESH)
    pl.semaphore_signal(barrier, inc=1, device_id={"expert": sib}, device_id_type=MESH)
    for i in range(1, n_a):
        pl.semaphore_signal(barrier, inc=1, device_id={"dp": ((dd // n_b + i) % n_a) * n_b + dd % n_b}, device_id_type=MESH)
    for i in range(1, n_b):
        pl.semaphore_signal(barrier, inc=1, device_id={"dp": dd // n_b * n_b + (dd % n_b + i) % n_b}, device_id_type=MESH)
    arrivals = n_a + n_b - 1 + jnp.where(z > 0, 1, 0) + jnp.where(z < n_z - 1, 1, 0)
    pl.semaphore_wait(barrier, arrivals)

    full = (PT, X, G)
    own = (PT.at[me], tok, cot)

    def hop(k, d, src, mine):
        there = me + (CORES if d == 0 else -CORES)
        return pltpu.make_async_remote_copy(
            src_ref=own[k] if mine else full[k].at[src],
            dst_ref=full[k].at[src],
            send_sem=chain_s.at[k, d, src],
            recv_sem=blk_r.at[k, src],
            device_id={"expert": there},
            device_id_type=MESH,
        )

    def across(k, src, mine):
        return pltpu.make_async_remote_copy(
            src_ref=own[k] if mine else full[k].at[src],
            dst_ref=full[k].at[src],
            send_sem=sib_s.at[k, src],
            recv_sem=blk_r.at[k, src],
            device_id={"expert": sib},
            device_id_type=MESH,
        )

    def can(d):
        return z < n_z - 1 if d == 0 else z > 0

    for k in range(3):
        for d in range(2):
            @pl.when(can(d))
            def _():
                hop(k, d, me, True).start()
        across(k, me, True).start()
    local = [
        pltpu.make_async_copy(tok, X.at[me], lsem.at[0]),
        pltpu.make_async_copy(cot, G.at[me], lsem.at[1]),
        pltpu.make_async_copy(wg_in.at[0], WG, lsem.at[2]),
        pltpu.make_async_copy(wu_in.at[0], WU, lsem.at[3]),
        pltpu.make_async_copy(wd_in.at[0], WD, lsem.at[4]),
    ]
    for copy in local:
        copy.start()
    for copy in local:
        copy.wait()

    pair = CORES * rows

    def base(zz):
        return pl.multiple_of(zz * pair, pair)

    def forward_tokens(zz, d):
        for k in range(2):
            across(k, zz * CORES + (1 - c), False).wait_recv()
        x = X[pl.ds(zz * CORES, CORES)].reshape(pair, width)
        GU[d, :, :hid] = jnp.dot(x, WG[...], preferred_element_type=jnp.float32)
        GU[d, :, hid:] = jnp.dot(x, WU[...], preferred_element_type=jnp.float32)
        XT[:, pl.ds(base(zz), pair)] = x.T

    def forward_cots(zz, d):
        across(2, zz * CORES + (1 - c), False).wait_recv()
        at = base(zz)
        parts = []
        for h in range(CORES):
            p = PT[zz * CORES + h, pl.ds(me, 1), :]
            p = jnp.broadcast_to(p, (rows, rows)).T[:, :1]
            parts.append((p * G[zz * CORES + h].astype(jnp.float32)).astype(jnp.bfloat16))
        scaled = jnp.concatenate(parts, axis=0)
        S[pl.ds(at, pair), :] = scaled
        gh = lax.dot_general(scaled, WD[...], (((1,), (1,)), ((), ())), preferred_element_type=jnp.float32)
        gate, up = GU[d, :, :hid], GU[d, :, hid:]
        sigma = jax.nn.sigmoid(gate)
        active = gate * sigma
        GG[pl.ds(at, pair), :hid] = (gh * up * sigma * (1.0 + gate * (1.0 - sigma))).astype(jnp.bfloat16)
        GG[pl.ds(at, pair), hid:] = (gh * active).astype(jnp.bfloat16)
        HT[:, pl.ds(at, pair)] = (active * up).astype(jnp.bfloat16).T

    def both(s, work):
        @pl.loop(0, 2)
        def _(d):
            zz = jnp.where(d == 0, z - s, z + s)

            @pl.when((zz >= 0) & (zz < n_z) & ((s > 0) | (d == 0)))
            def _():
                work(zz, d)

    def pass_on(s, kinds):
        for k in kinds:
            for d in range(2):
                zz = z - s if d == 0 else z + s
                src = zz * CORES + c

                @pl.when((zz >= 0) & (zz < n_z))
                def _():
                    hop(k, d, src, False).wait_recv()

                    @pl.when(can(d))
                    def _():
                        hop(k, d, src, False).start()

                    across(k, src, False).start()

    @pl.loop(0, n_z)
    def _(s):
        @pl.when(s > 0)
        def _():
            pass_on(s, (0, 1))

        both(s, forward_tokens)

        @pl.when(s > 0)
        def _():
            pass_on(s, (2,))

        both(s, forward_cots)

    piece, hpiece = width // n_d, hid // n_d
    chunk = max(piece, min(256, width))
    n_c = width // chunk
    hchunk, per = hid // n_c, chunk // piece
    half = width // 2

    def index(p, second, first):
        return second * n_b + first if p == 0 else first * n_b + second

    def first_of(p, j):
        return j % n_b if p == 0 else j // n_b

    def second_of(p, j):
        return j // n_b if p == 0 else j % n_b

    def mpiece(p, j):
        return MB.at[p, pl.ds(pl.multiple_of(j * piece, piece), piece)]

    def one(p, t, j):
        mine, there = first_of(p, dd), second_of(p, j)
        return pltpu.make_async_remote_copy(
            src_ref=mpiece(p, j) if t == 0 else DB.at[p, j],
            dst_ref=(MR if t == 0 else DR).at[p, mine, there],
            send_sem=one_s.at[p, t, j],
            recv_sem=one_r.at[p, t, mine, there],
            device_id={"dp": index(p, second_of(p, dd), first_of(p, j))},
            device_id_type=MESH,
        )

    def one_from(p, t, first, second):
        dst = (MR if t == 0 else DR).at[p, first, second]
        return pltpu.make_async_remote_copy(
            src_ref=dst, dst_ref=dst,
            send_sem=one_s.at[p, t, 0],
            recv_sem=one_r.at[p, t, first, second],
            device_id={"dp": index(p, second_of(p, dd), first)},
            device_id_type=MESH,
        )

    def two(p, t, second, slot):
        return pltpu.make_async_remote_copy(
            src_ref=(MP if t == 0 else DP).at[p, second],
            dst_ref=(MQ if t == 0 else DQ).at[p, slot],
            send_sem=two_s.at[p, t, second],
            recv_sem=two_r.at[p, t, slot],
            device_id={"dp": index(p, second, first_of(p, dd))},
            device_id_type=MESH,
        )

    @pl.loop(0, n_c)
    def _(i):
        if per == 1:
            step_a, step_b = n_a - 1 - i // n_b, n_b - 1 - i % n_b
            cc = ((dd // n_b + step_a) % n_a) * n_b + (dd % n_b + step_b) % n_b
        else:
            cc = (dd // per + 1 + i) % n_c
        at = pl.multiple_of(cc * chunk, chunk)
        hat = pl.multiple_of(cc * hchunk, hchunk)
        up_gate = jnp.dot(
            XT[pl.ds(at, chunk), :], GG[...], preferred_element_type=jnp.float32
        ).astype(jnp.bfloat16)
        for p in range(2):
            MB[p, pl.ds(at, chunk), :] = up_gate[:, p * hid : (p + 1) * hid]
        for t in range(2):
            if t == 1:
                down = jnp.dot(
                    HT[pl.ds(hat, hchunk), :], S[...], preferred_element_type=jnp.float32
                ).astype(jnp.bfloat16)
                for p in range(2):
                    for q in range(per):
                        DB[p, cc * per + q] = down[q * hpiece : (q + 1) * hpiece, p * half : (p + 1) * half]
            for p in range(2):
                for q in range(per):
                    j = cc * per + q

                    @pl.when(first_of(p, j) != first_of(p, dd))
                    def _():
                        one(p, t, j).start()

    def partial(p, t, second):
        first = first_of(p, dd)
        count = n_b if p == 0 else n_a
        j = index(p, second, first)
        total = (mpiece(p, j)[...] if t == 0 else DB[p, j]).astype(jnp.float32)
        for i in range(1, count):
            other = (first + i) % count
            one_from(p, t, other, second).wait_recv()
            total = total + (MR if t == 0 else DR)[p, other, second].astype(jnp.float32)
        return total

    for t in range(2):
        for p in range(2):
            count = n_a if p == 0 else n_b

            @pl.loop(1, count)
            def _(i):
                second = (second_of(p, dd) + i) % count
                (MP if t == 0 else DP)[p, second] = partial(p, t, second).astype(jnp.bfloat16)
                two(p, t, second, second_of(p, dd)).start()

    for t in range(2):
        for p in range(2):
            count = n_a if p == 0 else n_b
            mine = second_of(p, dd)
            total = partial(p, t, mine)
            for i in range(1, count):
                other = (mine + i) % count
                two(p, t, other, other).wait_recv()
                total = total + (MQ if t == 0 else DQ)[p, other].astype(jnp.float32)
            if t == 0:
                (out_g, out_u)[p][0] = total.astype(jnp.bfloat16)
            else:
                out_d[0, :, p * half : (p + 1) * half] = total.astype(jnp.bfloat16)

    for p in range(2):
        for t in range(2):
            @pl.loop(0, n_d)
            def _(j):
                @pl.when(first_of(p, j) != first_of(p, dd))
                def _():
                    one(p, t, j).wait_send()

            count = n_a if p == 0 else n_b

            @pl.loop(1, count)
            def _(i):
                two(p, t, (second_of(p, dd) + i) % count, second_of(p, dd)).wait_send()

    @pl.loop(0, n_z)
    def _(s):
        for k in range(3):
            for d in range(2):
                zz = z - s if d == 0 else z + s
                src = zz * CORES + c

                @pl.when((zz >= 0) & (zz < n_z) & can(d))
                def _():
                    hop(k, d, src, False).wait_send()

            across(k, s * CORES + c, False).wait_send()


def solution(mesh):
    n_e, n_d = mesh.shape["expert"], mesh.shape["dp"]
    n_b = max(b for b in range(1, n_d + 1) if n_d % b == 0 and b * b <= n_d)
    n_a = n_d // n_b

    def step(tokens, out_grad, expert_ids, gate_probs, w_gate, w_up, w_down):
        rows, width = tokens.shape
        hid = w_gate.shape[2]
        total = n_e * rows
        lanes = -(-n_e // 8) * 8
        bf, f32 = jnp.bfloat16, jnp.float32
        vmem = pl.BlockSpec(memory_space=pltpu.VMEM)
        hbm = pl.BlockSpec(memory_space=pltpu.HBM)
        piece, hpiece = width // n_d, hid // n_d
        dma = pltpu.SemaphoreType.DMA
        scratch = [
            ((n_e, rows, width), bf),
            ((n_e, rows, width), bf),
            ((n_e, lanes, rows), f32),
            ((width, hid), bf),
            ((width, hid), bf),
            ((hid, width), bf),
            ((2, CORES * rows, 2 * hid), f32),
            ((width, total), bf),
            ((hid, total), bf),
            ((total, 2 * hid), bf),
            ((total, width), bf),
            ((2, width, hid), bf),
            ((2, n_d, hpiece, width // 2), bf),
            ((2, n_a, n_a, piece, hid), bf),
            ((2, n_a, n_a, hpiece, width // 2), bf),
            ((2, n_a, piece, hid), bf),
            ((2, n_a, hpiece, width // 2), bf),
            ((2, n_a, piece, hid), bf),
            ((2, n_a, hpiece, width // 2), bf),
        ]
        held = sum(math.prod(shape) * jnp.dtype(kind).itemsize for shape, kind in scratch)
        return pl.pallas_call(
            functools.partial(kernel, n_e, n_a, n_b),
            out_shape=(
                jax.ShapeDtypeStruct((1, piece, hid), bf),
                jax.ShapeDtypeStruct((1, piece, hid), bf),
                jax.ShapeDtypeStruct((1, hpiece, width), bf),
            ),
            in_specs=[hbm, hbm, vmem, vmem, hbm, hbm, hbm],
            out_specs=(vmem, vmem, vmem),
            scratch_shapes=[pltpu.VMEM(shape, kind) for shape, kind in scratch]
            + [
                dma((5,)),
                dma((3, 2, n_e)),
                dma((3, n_e)),
                dma((3, n_e)),
                dma((2, 2, n_d)),
                dma((2, 2, n_a, n_a)),
                dma((2, 2, n_a)),
                dma((2, 2, n_a)),
            ],
            compiler_params=pltpu.CompilerParams(
                collective_id=0, has_side_effects=True, vmem_limit_bytes=held + (10 << 20)
            ),
        )(tokens, out_grad, expert_ids.T, gate_probs.T, w_gate, w_up, w_down)

    spread = P(("expert", "dp"), None)
    return jax.shard_map(
        step,
        mesh=mesh,
        in_specs=(spread, spread, spread, spread) + (P("expert", None, None),) * 3,
        out_specs=(P("expert", "dp", None),) * 3,
        check_vma=False,
    )
```

time: 77.4 us -> 73.1 us (0.944)
  Pallas kernels: 73.2 us -> 63.3 us
  local copies, waits for them, and re-layouts: 3.34 us -> 8.68 us
    pallas_call x1, Pallas kernels: 73.2 us -> 63.3 us  [step(): pl.pallas_call(functools.partial(kernel, n_e, n_a, n_b), out_shape=(jax.S...]
    unnamed x7 -> x17, local copies, waits for them, and re-layouts: 3.34 us -> 8.68 us
where the time goes in v2:
time: 73.1 us; the launch traced here: 72.6 us
  Pallas kernels  63.3 us (87%)
  local copies, waits for them, and re-layouts  8.68 us (12%)
    pallas_call x1, Pallas kernels, step(): pl.pallas_call(functools.partial(kernel, n_e, n_a, n_b), out_shape=(jax.S...  63.3 us
    unnamed x17, local copies, waits for them, and re-layouts  8.68 us

profile of v2, /device:TPU:0, one launch (start us, length us, event | category | flops | bytes accessed | tf_op | source)
XLA Modules:
  0.0 72.6 jit_solution(10151511885107011577)
XLA Ops:
  0.6 0.0 copy-start.5
  0.6 0.7 copy-done.5
  1.3 0.0 copy-start
  1.3 1.1 %copy-done = bf16[1,1024,384]{2,1,0:T(8,128)(2,1)S(1)} copy-done((bf16[1,1024,384]{2,1,0:T(8,128)(2,1)S(1)}, bf16[1,1024,384]{2,1,0:T(8,128)(2,1)}, u32[]{:S(2)}) %copy-start) | copy-done | bytes 786456
  2.4 0.0 copy-start.1
  2.5 1.1 %copy-done.1 = bf16[1,1024,384]{2,1,0:T(8,128)(2,1)S(1)} copy-done((bf16[1,1024,384]{2,1,0:T(8,128)(2,1)S(1)}, bf16[1,1024,384]{2,1,0:T(8,128)(2,1)}, u32[]{:S(2)}) %copy-start.1) | copy-done | bytes 786456
  3.6 0.0 copy-start.2
  3.6 1.1 %copy-done.2 = bf16[1,384,1024]{2,1,0:T(8,128)(2,1)S(1)} copy-done((bf16[1,384,1024]{2,1,0:T(8,128)(2,1)S(1)}, bf16[1,384,1024]{2,1,0:T(8,128)(2,1)}, u32[]{:S(2)}) %copy-start.2) | copy-done | bytes 786456
  4.7 0.0 copy-start.3
  4.7 0.9 %copy-done.3 = bf16[128,1024]{1,0:T(8,128)(2,1)S(1)} copy-done((bf16[128,1024]{1,0:T(8,128)(2,1)S(1)}, bf16[128,1024]{1,0:T(8,128)(2,1)}, u32[]{:S(2)}) %copy-start.3) | copy-done | bytes 262168
  5.7 0.0 copy-start.4
  5.7 0.9 %copy-done.4 = bf16[128,1024]{1,0:T(8,128)(2,1)S(1)} copy-done((bf16[128,1024]{1,0:T(8,128)(2,1)S(1)}, bf16[128,1024]{1,0:T(8,128)(2,1)}, u32[]{:S(2)}) %copy-start.4) | copy-done | bytes 262168
  6.6 0.0 copy-start.6
  6.6 0.7 copy-done.6
  7.3 63.3 %shard_map.94 = (bf16[1,256,384]{2,1,0:T(8,128)(2,1)S(1)}, bf16[1,256,384]{2,1,0:T(8,128)(2,1)S(1)}, bf16[1,96,1024]{2,1,0:T(8,128)(2,1)S(1)}) custom-call(bf16[128,1024]{1,0:T(8,128)(2,1)S(1)} %copy-done.3, bf16[128,1024]{1,0:T(8,128)(2,1)S(1)} %copy-done.4, s32[3,128]{1,0:T(4,128)S(1)} %bitcast.2, f32[3,128]{1,0:T(4,128)S(1)} %bitcast.3, ...), custom_call_target="tpu_custom_call" | custom-call | tf_op jit(solution)/shard_map/pallas_call | solution.py:345
  70.6 0.7 copy.13
  71.2 0.7 copy.14
  71.9 0.7 copy.15
Async XLA Ops:
  0.6 0.7 copy-start.5
  1.3 1.1 %copy-start = (bf16[1,1024,384]{2,1,0:T(8,128)(2,1)S(1)}, bf16[1,1024,384]{2,1,0:T(8,128)(2,1)}, u32[]{:S(2)}) copy-start(bf16[1,1024,384]{2,1,0:T(8,128)(2,1)} %wg_in.1) | copy-start | bytes 2359300
  2.4 1.1 %copy-start.1 = (bf16[1,1024,384]{2,1,0:T(8,128)(2,1)S(1)}, bf16[1,1024,384]{2,1,0:T(8,128)(2,1)}, u32[]{:S(2)}) copy-start(bf16[1,1024,384]{2,1,0:T(8,128)(2,1)} %wu_in.1) | copy-start | bytes 2359300
  3.6 1.1 %copy-start.2 = (bf16[1,384,1024]{2,1,0:T(8,128)(2,1)S(1)}, bf16[1,384,1024]{2,1,0:T(8,128)(2,1)}, u32[]{:S(2)}) copy-start(bf16[1,384,1024]{2,1,0:T(8,128)(2,1)} %wd_in.1) | copy-start | bytes 2359300
  4.7 0.9 %copy-start.3 = (bf16[128,1024]{1,0:T(8,128)(2,1)S(1)}, bf16[128,1024]{1,0:T(8,128)(2,1)}, u32[]{:S(2)}) copy-start(bf16[128,1024]{1,0:T(8,128)(2,1)} %tok.1) | copy-start | bytes 786436
  5.7 0.9 %copy-start.4 = (bf16[128,1024]{1,0:T(8,128)(2,1)S(1)}, bf16[128,1024]{1,0:T(8,128)(2,1)}, u32[]{:S(2)}) copy-start(bf16[128,1024]{1,0:T(8,128)(2,1)} %cot.1) | copy-start | bytes 786436
  6.6 0.7 copy-start.6

commit v3 on v2

--- a/solution.py
+++ b/solution.py
@@ -14,26 +14,20 @@
 
 def kernel(
     n_e, n_a, n_b,
-    tok, cot, ids, probs, wg_in, wu_in, wd_in,
+    tok, cot, ids_in, probs_in, wg_in, wu_in, wd_in,
     out_g, out_u, out_d,
-    X, G, PT, WG, WU, WD, GU, XT, HT, GG, S, MB, DB, MR, DR, MP, DP, MQ, DQ,
+    ids, probs, X, G, PT, WG, WU, WD, GU, XT, HT, GG, S, MB, DB, MR, DR, MP, DP, MQ, DQ,
     lsem, chain_s, sib_s, blk_r, one_s, one_r, two_s, two_r,
 ):
     n_d = n_a * n_b
     rows, width = tok.shape
     hid = wg_in.shape[2]
-    top = ids.shape[0]
+    top = ids_in.shape[0]
     n_z = n_e // CORES
     me = lax.axis_index("expert")
     dd = lax.axis_index("dp")
     z, c = me // CORES, me % CORES
     sib = z * CORES + (1 - c)
-
-    erow = lax.broadcasted_iota(jnp.int32, PT.shape[1:], 0)
-    table = jnp.zeros(PT.shape[1:], jnp.float32)
-    for k in range(top):
-        table = table + jnp.where(ids[k : k + 1, :] == erow, probs[k : k + 1, :], 0.0)
-    PT[me] = table
 
     barrier = pltpu.get_barrier_semaphore()
     for step in (-1, 1):
@@ -45,6 +39,20 @@
         pl.semaphore_signal(barrier, inc=1, device_id={"dp": ((dd // n_b + i) % n_a) * n_b + dd % n_b}, device_id_type=MESH)
     for i in range(1, n_b):
         pl.semaphore_signal(barrier, inc=1, device_id={"dp": dd // n_b * n_b + (dd % n_b + i) % n_b}, device_id_type=MESH)
+    small = [
+        pltpu.make_async_copy(ids_in, ids, lsem.at[5]),
+        pltpu.make_async_copy(probs_in, probs, lsem.at[6]),
+    ]
+    for copy in small:
+        copy.start()
+    for copy in small:
+        copy.wait()
+    erow = lax.broadcasted_iota(jnp.int32, PT.shape[1:], 0)
+    table = jnp.zeros(PT.shape[1:], jnp.float32)
+    for k in range(top):
+        table = table + jnp.where(ids[k : k + 1, :] == erow, probs[k : k + 1, :], 0.0)
+    PT[me] = table
+
     arrivals = n_a + n_b - 1 + jnp.where(z > 0, 1, 0) + jnp.where(z < n_z - 1, 1, 0)
     pl.semaphore_wait(barrier, arrivals)
 
@@ -305,6 +313,27 @@
             across(k, s * CORES + c, False).wait_send()
 
 
+def copy_out(*refs):
+    n = len(refs) // 2
+    copies = [pltpu.make_async_copy(refs[i], refs[n + i], refs[-1].at[i]) for i in range(n)]
+    for copy in copies:
+        copy.start()
+    for copy in copies:
+        copy.wait()
+
+
+def write_out(arrays):
+    anywhere = pl.BlockSpec(memory_space=pl.ANY)
+    return pl.pallas_call(
+        copy_out,
+        out_shape=tuple(jax.ShapeDtypeStruct(x.shape, x.dtype) for x in arrays),
+        in_specs=[anywhere] * len(arrays),
+        out_specs=(anywhere,) * len(arrays),
+        scratch_shapes=[pltpu.SemaphoreType.DMA((len(arrays),))],
+        compiler_params=pltpu.CompilerParams(vmem_limit_bytes=1 << 20),
+    )(*arrays)
+
+
 def solution(mesh):
     n_e, n_d = mesh.shape["expert"], mesh.shape["dp"]
     n_b = max(b for b in range(1, n_d + 1) if n_d % b == 0 and b * b <= n_d)
@@ -321,6 +350,8 @@
         piece, hpiece = width // n_d, hid // n_d
         dma = pltpu.SemaphoreType.DMA
         scratch = [
+            (expert_ids.shape[::-1], expert_ids.dtype),
+            (gate_probs.shape[::-1], gate_probs.dtype),
             ((n_e, rows, width), bf),
             ((n_e, rows, width), bf),
             ((n_e, lanes, rows), f32),
@@ -342,18 +373,19 @@
             ((2, n_a, hpiece, width // 2), bf),
         ]
         held = sum(math.prod(shape) * jnp.dtype(kind).itemsize for shape, kind in scratch)
-        return pl.pallas_call(
+        args = (tokens, out_grad, expert_ids.T, gate_probs.T, w_gate, w_up, w_down)
+        made = pl.pallas_call(
             functools.partial(kernel, n_e, n_a, n_b),
             out_shape=(
                 jax.ShapeDtypeStruct((1, piece, hid), bf),
                 jax.ShapeDtypeStruct((1, piece, hid), bf),
                 jax.ShapeDtypeStruct((1, hpiece, width), bf),
             ),
-            in_specs=[hbm, hbm, vmem, vmem, hbm, hbm, hbm],
+            in_specs=[hbm] * 7,
             out_specs=(vmem, vmem, vmem),
             scratch_shapes=[pltpu.VMEM(shape, kind) for shape, kind in scratch]
             + [
-                dma((5,)),
+                dma((7,)),
                 dma((3, 2, n_e)),
                 dma((3, n_e)),
                 dma((3, n_e)),
@@ -365,7 +397,8 @@
             compiler_params=pltpu.CompilerParams(
                 collective_id=0, has_side_effects=True, vmem_limit_bytes=held + (10 << 20)
             ),
-        )(tokens, out_grad, expert_ids.T, gate_probs.T, w_gate, w_up, w_down)
+        )(*(pltpu.with_memory_space_constraint(x, pltpu.HBM) for x in args))
+        return write_out(made)
 
     spread = P(("expert", "dp"), None)
     return jax.shard_map(

time: 73.1 us -> 65.4 us (0.89)
  local copies, waits for them, and re-layouts: 8.68 us -> 0 us
  Pallas kernels: 63.3 us -> 64.5 us
    unnamed x17 -> x0, local copies, waits for them, and re-layouts: 8.68 us -> none
    pallas_call x0 -> x1, Pallas kernels: none -> 0.83 us  [write_out(): pl.pallas_call(copy_out, out_shape=tuple((jax.ShapeDtypeStruct(x.shape, x...]
where the time goes in v3:
time: 65.4 us; the launch traced here: 65.1 us
  Pallas kernels  64.5 us (99%)
    pallas_call x1, Pallas kernels, step(): pl.pallas_call(functools.partial(kernel, n_e, n_a, n_b), out_shape=(jax.S...  63.7 us

profile of v3, /device:TPU:0, one launch (start us, length us, event | category | flops | bytes accessed | tf_op | source)
XLA Modules:
  0.0 65.1 jit_solution(9154226429300897714)
XLA Ops:
  0.6 63.7 %shard_map.94 = (bf16[1,256,384]{2,1,0:T(8,128)(2,1)S(1)}, bf16[1,256,384]{2,1,0:T(8,128)(2,1)S(1)}, bf16[1,96,1024]{2,1,0:T(8,128)(2,1)S(1)}) custom-call(bf16[128,1024]{1,0:T(8,128)(2,1)} %tok.1, bf16[128,1024]{1,0:T(8,128)(2,1)} %cot.1, s32[3,128]{1,0:T(4,128)} %bitcast.2, f32[3,128]{1,0:T(4,128)} %bitcast.3, bf16[1,1024,384]{2,1,0:T(8,128)(2,1)} %wg_in.1, ...), custom_call_target="tpu_custom_call" | custom-call | tf_op jit(solution)/shard_map/pallas_call | solution.py:377
  64.3 0.8 %shard_map.95 = (bf16[1,256,384]{2,1,0:T(8,128)(2,1)}, bf16[1,256,384]{2,1,0:T(8,128)(2,1)}, bf16[1,96,1024]{2,1,0:T(8,128)(2,1)}) custom-call(bf16[1,256,384]{2,1,0:T(8,128)(2,1)S(1)} %get-tuple-element.6.refs_0_, bf16[1,256,384]{2,1,0:T(8,128)(2,1)S(1)} %get-tuple-element.7.refs_1_, bf16[1,96,1024]{2,1,0:T(8,128)(2,1)S(1)} %get-tuple-element.8.refs_2_), custom_call_target="tpu_custom_call" | custom-call | tf_op jit(solution)/shard_map/pallas_call | solution.py:327

commit v4 on v3

v4 whole, which is shorter than its diff:
```python
import functools
import math

import jax
import jax.numpy as jnp
from jax import lax
from jax.experimental import pallas as pl
from jax.experimental.pallas import tpu as pltpu
from jax.sharding import PartitionSpec as P

MESH = pl.DeviceIdType.MESH
CORES = 2
QUARTERS = 4


def kernel(
    n_e, n_a, n_b,
    tok, cot, ids_in, probs_in, wg_in, wu_in, wd_in,
    out_g, out_u, out_d,
    ids, probs, X, G, PT, WG, WU, WD, GU, GH, XT, HT, GG, S, MB, DB, MR, DR, MP, DP, MQ, DQ,
    lsem, chain_s, sib_s, blk_r, one_s, one_r, two_s, two_r,
):
    n_d = n_a * n_b
    rows, width = tok.shape
    hid = wg_in.shape[2]
    top = ids_in.shape[0]
    n_z = n_e // CORES
    me = lax.axis_index("expert")
    dd = lax.axis_index("dp")
    z, c = me // CORES, me % CORES
    sib = z * CORES + (1 - c)

    barrier = pltpu.get_barrier_semaphore()
    for step in (-1, 1):
        @pl.when(jnp.logical_and(z + step >= 0, z + step < n_z))
        def _():
            pl.semaphore_signal(barrier, inc=1, device_id={"expert": me + step * CORES}, device_id_type=MESH)
    pl.semaphore_signal(barrier, inc=1, device_id={"expert": sib}, device_id_type=MESH)
    for i in range(1, n_a):
        pl.semaphore_signal(barrier, inc=1, device_id={"dp": ((dd // n_b + i) % n_a) * n_b + dd % n_b}, device_id_type=MESH)
    for i in range(1, n_b):
        pl.semaphore_signal(barrier, inc=1, device_id={"dp": dd // n_b * n_b + (dd % n_b + i) % n_b}, device_id_type=MESH)
    small = [
        pltpu.make_async_copy(ids_in, ids, lsem.at[5]),
        pltpu.make_async_copy(probs_in, probs, lsem.at[6]),
    ]
    for copy in small:
        copy.start()
    for copy in small:
        copy.wait()
    erow = lax.broadcasted_iota(jnp.int32, PT.shape[1:], 0)
    table = jnp.zeros(PT.shape[1:], jnp.float32)
    for k in range(top):
        table = table + jnp.where(ids[k : k + 1, :] == erow, probs[k : k + 1, :], 0.0)
    PT[me] = table

    arrivals = n_a + n_b - 1 + jnp.where(z > 0, 1, 0) + jnp.where(z < n_z - 1, 1, 0)
    pl.semaphore_wait(barrier, arrivals)

    wide = width // QUARTERS

    def full(k, src):
        if k < 2:
            return (PT, X)[k].at[src]
        return G.at[src, :, pl.ds((k - 2) * wide, wide)]

    def own(k):
        if k < 2:
            return (PT.at[me], tok)[k]
        return cot.at[:, pl.ds((k - 2) * wide, wide)]

    def hop(k, d, src, mine):
        there = me + (CORES if d == 0 else -CORES)
        return pltpu.make_async_remote_copy(
            src_ref=own(k) if mine else full(k, src),
            dst_ref=full(k, src),
            send_sem=chain_s.at[k, d, src],
            recv_sem=blk_r.at[k, src],
            device_id={"expert": there},
            device_id_type=MESH,
        )

    def across(k, src, mine):
        return pltpu.make_async_remote_copy(
            src_ref=own(k) if mine else full(k, src),
            dst_ref=full(k, src),
            send_sem=sib_s.at[k, src],
            recv_sem=blk_r.at[k, src],
            device_id={"expert": sib},
            device_id_type=MESH,
        )

    def can(d):
        return z < n_z - 1 if d == 0 else z > 0

    kinds = 2 + QUARTERS
    for k in range(kinds):
        for d in range(2):
            @pl.when(can(d) if k < 2 else z == (0 if d == 0 else n_z - 1))
            def _():
                hop(k, d, me, True).start()
        across(k, me, True).start()
    local = [
        pltpu.make_async_copy(tok, X.at[me], lsem.at[0]),
        pltpu.make_async_copy(cot, G.at[me], lsem.at[1]),
        pltpu.make_async_copy(wg_in.at[0], WG, lsem.at[2]),
        pltpu.make_async_copy(wu_in.at[0], WU, lsem.at[3]),
        pltpu.make_async_copy(wd_in.at[0], WD, lsem.at[4]),
    ]
    for copy in local:
        copy.start()
    for copy in local:
        copy.wait()

    pair = CORES * rows

    def base(zz):
        return pl.multiple_of(zz * pair, pair)

    def forward_tokens(zz):
        for k in range(2):
            across(k, zz * CORES + (1 - c), False).wait_recv()
        at = base(zz)
        x = X[pl.ds(zz * CORES, CORES)].reshape(pair, width)
        gate = jnp.dot(x, WG[...], preferred_element_type=jnp.float32)
        up = jnp.dot(x, WU[...], preferred_element_type=jnp.float32)
        sigma = jax.nn.sigmoid(gate)
        active = gate * sigma
        GU[pl.ds(at, pair), :hid] = up * sigma * (1.0 + gate * (1.0 - sigma))
        GU[pl.ds(at, pair), hid:] = active
        HT[:, pl.ds(at, pair)] = (active * up).astype(jnp.bfloat16).T
        XT[:, pl.ds(at, pair)] = x.T

    def forward_cots(zz, q):
        across(2 + q, zz * CORES + (1 - c), False).wait_recv()
        at = base(zz)
        cols = slice(q * wide, (q + 1) * wide)
        parts = []
        for h in range(CORES):
            p = PT[zz * CORES + h, pl.ds(me, 1), :]
            p = jnp.broadcast_to(p, (rows, rows)).T[:, :1]
            parts.append((p * G[zz * CORES + h, :, cols].astype(jnp.float32)).astype(jnp.bfloat16))
        scaled = jnp.concatenate(parts, axis=0)
        S[pl.ds(at, pair), cols] = scaled
        gh = lax.dot_general(scaled, WD[:, cols], (((1,), (1,)), ((), ())), preferred_element_type=jnp.float32)
        if q > 0:
            gh = gh + GH[pl.ds(at, pair), :]
        if q < QUARTERS - 1:
            GH[pl.ds(at, pair), :] = gh
        else:
            GG[pl.ds(at, pair), :hid] = (gh * GU[pl.ds(at, pair), :hid]).astype(jnp.bfloat16)
            GG[pl.ds(at, pair), hid:] = (gh * GU[pl.ds(at, pair), hid:]).astype(jnp.bfloat16)

    def both(s, work):
        @pl.loop(0, 2)
        def _(d):
            zz = jnp.where(d == 0, z - s, z + s)

            @pl.when((zz >= 0) & (zz < n_z) & ((s > 0) | (d == 0)))
            def _():
                work(zz)

    def pass_on(s, group, after):
        for k in group:
            for d in range(2):
                zz = z - s if d == 0 else z + s
                src = zz * CORES + c

                @pl.when((zz >= 0) & (zz < n_z))
                def _():
                    hop(k, d, src, False).wait_recv()

                    @pl.when(can(d))
                    def _():
                        hop(k, d, src, False).start()

                    across(k, src, False).start()

                if k == group[-1] and after < kinds:
                    @pl.when((zz == (0 if d == 0 else n_z - 1)) & can(d))
                    def _():
                        hop(after, d, me, True).start()

    @pl.loop(0, n_z)
    def _(s):
        @pl.when(s > 0)
        def _():
            pass_on(s, (0, 1), 2)

        both(s, forward_tokens)

    piece, hpiece = width // n_d, hid // n_d
    chunk = max(piece, min(256, width))
    n_c = width // chunk
    hchunk, per = hid // n_c, chunk // piece

    def index(p, second, first):
        return second * n_b + first if p == 0 else first * n_b + second

    def first_of(p, j):
        return j % n_b if p == 0 else j // n_b

    def second_of(p, j):
        return j // n_b if p == 0 else j % n_b

    def mpiece(p, j):
        return MB.at[p, pl.ds(pl.multiple_of(j * piece, piece), piece)]

    def path(t):
        return t % 2

    def buffers(t):
        return (MR.at[t], MP.at[t], MQ.at[t]) if t < 2 else (DR.at[t - 2], DP.at[t - 2], DQ.at[t - 2])

    def source(t, j):
        return mpiece(t, j) if t < 2 else DB.at[t - 2, j]

    def one(t, j):
        p = path(t)
        mine, there = first_of(p, dd), second_of(p, j)
        return pltpu.make_async_remote_copy(
            src_ref=source(t, j),
            dst_ref=buffers(t)[0].at[mine, there],
            send_sem=one_s.at[t, j],
            recv_sem=one_r.at[t, mine, there],
            device_id={"dp": index(p, second_of(p, dd), first_of(p, j))},
            device_id_type=MESH,
        )

    def one_from(t, first, second):
        dst = buffers(t)[0].at[first, second]
        return pltpu.make_async_remote_copy(
            src_ref=dst, dst_ref=dst,
            send_sem=one_s.at[t, 0],
            recv_sem=one_r.at[t, first, second],
            device_id={"dp": index(path(t), second_of(path(t), dd), first)},
            device_id_type=MESH,
        )

    def two(t, second, slot):
        p = path(t)
        return pltpu.make_async_remote_copy(
            src_ref=buffers(t)[1].at[second],
            dst_ref=buffers(t)[2].at[slot],
            send_sem=two_s.at[t, second],
            recv_sem=two_r.at[t, slot],
            device_id={"dp": index(p, second, first_of(p, dd))},
            device_id_type=MESH,
        )

    def partial(t, second):
        p = path(t)
        first = first_of(p, dd)
        count = n_b if p == 0 else n_a
        total = source(t, index(p, second, first))[...].astype(jnp.float32)
        for i in range(1, count):
            other = (first + i) % count
            one_from(t, other, second).wait_recv()
            total = total + buffers(t)[0][other, second].astype(jnp.float32)
        return total

    def seconds(t):
        return n_a if path(t) == 0 else n_b

    def relay(t):
        @pl.loop(1, seconds(t))
        def _(i):
            second = (second_of(path(t), dd) + i) % seconds(t)
            buffers(t)[1][second] = partial(t, second).astype(jnp.bfloat16)
            two(t, second, second_of(path(t), dd)).start()

    def turn(i):
        if per == 1:
            step_a, step_b = n_a - 1 - i // n_b, n_b - 1 - i % n_b
            return ((dd // n_b + step_a) % n_a) * n_b + (dd % n_b + step_b) % n_b
        return (dd // per + 1 + i) % n_c

    def give(t, j):
        @pl.when(first_of(path(t), j) != first_of(path(t), dd))
        def _():
            one(t, j).start()

    def make_down(q):
        @pl.loop(0, n_c)
        def _(i):
            cc = turn(i)
            hat = pl.multiple_of(cc * hchunk, hchunk)
            down = jnp.dot(
                HT[pl.ds(hat, hchunk), :], S[:, q * wide : (q + 1) * wide], preferred_element_type=jnp.float32
            ).astype(jnp.bfloat16)
            for r in range(per):
                DB[q, cc * per + r] = down[r * hpiece : (r + 1) * hpiece]
            for r in range(per):
                give(2 + q, cc * per + r)

    for q in range(QUARTERS):
        @pl.loop(0, n_z)
        def _(s):
            @pl.when(s > 0)
            def _():
                pass_on(s, (2 + q,), 3 + q)

            both(s, functools.partial(forward_cots, q=q))

        if q < QUARTERS - 1:
            make_down(q)
        if q > 0:
            relay(1 + q)

    @pl.loop(0, n_c)
    def _(i):
        cc = turn(i)
        at = pl.multiple_of(cc * chunk, chunk)
        both_grads = jnp.dot(
            XT[pl.ds(at, chunk), :], GG[...], preferred_element_type=jnp.float32
        ).astype(jnp.bfloat16)
        for t in range(2):
            MB[t, pl.ds(at, chunk), :] = both_grads[:, t * hid : (t + 1) * hid]
        for t in range(2):
            for r in range(per):
                give(t, cc * per + r)

    make_down(QUARTERS - 1)
    for t in (0, 1, 1 + QUARTERS):
        relay(t)

    for t in tuple(range(2, 1 + QUARTERS)) + (0, 1, 1 + QUARTERS):
        mine = second_of(path(t), dd)
        total = partial(t, mine)
        for i in range(1, seconds(t)):
            other = (mine + i) % seconds(t)
            two(t, other, other).wait_recv()
            total = total + buffers(t)[2][other].astype(jnp.float32)
        if t < 2:
            (out_g, out_u)[t][0] = total.astype(jnp.bfloat16)
        else:
            out_d[0, :, (t - 2) * wide : (t - 1) * wide] = total.astype(jnp.bfloat16)

    for t in range(2 + QUARTERS):
        @pl.loop(0, n_d)
        def _(j):
            @pl.when(first_of(path(t), j) != first_of(path(t), dd))
            def _():
                one(t, j).wait_send()

        @pl.loop(1, seconds(t))
        def _(i):
            two(t, (second_of(path(t), dd) + i) % seconds(t), second_of(path(t), dd)).wait_send()

    @pl.loop(0, n_z)
    def _(s):
        for k in range(kinds):
            for d in range(2):
                zz = z - s if d == 0 else z + s
                src = zz * CORES + c

                @pl.when((zz >= 0) & (zz < n_z) & can(d))
                def _():
                    hop(k, d, src, False).wait_send()

            across(k, s * CORES + c, False).wait_send()


def copy_out(*refs):
    n = len(refs) // 2
    copies = [pltpu.make_async_copy(refs[i], refs[n + i], refs[-1].at[i]) for i in range(n)]
    for copy in copies:
        copy.start()
    for copy in copies:
        copy.wait()


def write_out(arrays):
    anywhere = pl.BlockSpec(memory_space=pl.ANY)
    return pl.pallas_call(
        copy_out,
        out_shape=tuple(jax.ShapeDtypeStruct(x.shape, x.dtype) for x in arrays),
        in_specs=[anywhere] * len(arrays),
        out_specs=(anywhere,) * len(arrays),
        scratch_shapes=[pltpu.SemaphoreType.DMA((len(arrays),))],
        compiler_params=pltpu.CompilerParams(vmem_limit_bytes=1 << 20),
    )(*arrays)


def solution(mesh):
    n_e, n_d = mesh.shape["expert"], mesh.shape["dp"]
    n_b = max(b for b in range(1, n_d + 1) if n_d % b == 0 and b * b <= n_d)
    n_a = n_d // n_b

    def step(tokens, out_grad, expert_ids, gate_probs, w_gate, w_up, w_down):
        rows, width = tokens.shape
        hid = w_gate.shape[2]
        total = n_e * rows
        lanes = -(-n_e // 8) * 8
        bf, f32 = jnp.bfloat16, jnp.float32
        vmem = pl.BlockSpec(memory_space=pltpu.VMEM)
        hbm = pl.BlockSpec(memory_space=pltpu.HBM)
        piece, hpiece = width // n_d, hid // n_d
        dma = pltpu.SemaphoreType.DMA
        scratch = [
            (expert_ids.shape[::-1], expert_ids.dtype),
            (gate_probs.shape[::-1], gate_probs.dtype),
            ((n_e, rows, width), bf),
            ((n_e, rows, width), bf),
            ((n_e, lanes, rows), f32),
            ((width, hid), bf),
            ((width, hid), bf),
            ((hid, width), bf),
            ((total, 2 * hid), f32),
            ((total, hid), f32),
            ((width, total), bf),
            ((hid, total), bf),
            ((total, 2 * hid), bf),
            ((total, width), bf),
            ((2, width, hid), bf),
            ((QUARTERS, n_d, hpiece, width // QUARTERS), bf),
            ((2, n_a, n_a, piece, hid), bf),
            ((QUARTERS, n_a, n_a, hpiece, width // QUARTERS), bf),
            ((2, n_a, piece, hid), bf),
            ((QUARTERS, n_a, hpiece, width // QUARTERS), bf),
            ((2, n_a, piece, hid), bf),
            ((QUARTERS, n_a, hpiece, width // QUARTERS), bf),
        ]
        held = sum(math.prod(shape) * jnp.dtype(kind).itemsize for shape, kind in scratch)
        args = (tokens, out_grad, expert_ids.T, gate_probs.T, w_gate, w_up, w_down)
        made = pl.pallas_call(
            functools.partial(kernel, n_e, n_a, n_b),
            out_shape=(
                jax.ShapeDtypeStruct((1, piece, hid), bf),
                jax.ShapeDtypeStruct((1, piece, hid), bf),
                jax.ShapeDtypeStruct((1, hpiece, width), bf),
            ),
            in_specs=[hbm] * 7,
            out_specs=(vmem, vmem, vmem),
            scratch_shapes=[pltpu.VMEM(shape, kind) for shape, kind in scratch]
            + [
                dma((7,)),
                dma((2 + QUARTERS, 2, n_e)),
                dma((2 + QUARTERS, n_e)),
                dma((2 + QUARTERS, n_e)),
                dma((2 + QUARTERS, n_d)),
                dma((2 + QUARTERS, n_a, n_a)),
                dma((2 + QUARTERS, n_a)),
                dma((2 + QUARTERS, n_a)),
            ],
            compiler_params=pltpu.CompilerParams(
                collective_id=0, has_side_effects=True, vmem_limit_bytes=held + (10 << 20)
            ),
        )(*(pltpu.with_memory_space_constraint(x, pltpu.HBM) for x in args))
        return write_out(made)

    spread = P(("expert", "dp"), None)
    return jax.shard_map(
        step,
        mesh=mesh,
        in_specs=(spread, spread, spread, spread) + (P("expert", None, None),) * 3,
        out_specs=(P("expert", "dp", None),) * 3,
        check_vma=False,
    )
```

time: 65.4 us -> 71.8 us (1.098)
  Pallas kernels: 64.5 us -> 70.9 us
    pallas_call x1, Pallas kernels: 63.7 us -> 70.1 us  [step(): pl.pallas_call(functools.partial(kernel, n_e, n_a, n_b), out_shape=(jax.S...]
where the time goes in v4:
time: 71.8 us; the launch traced here: 71.6 us
  Pallas kernels  70.9 us (99%)
    pallas_call x1, Pallas kernels, step(): pl.pallas_call(functools.partial(kernel, n_e, n_a, n_b), out_shape=(jax.S...  70.1 us

profile of v4, /device:TPU:0, one launch (start us, length us, event | category | flops | bytes accessed | tf_op | source)
XLA Modules:
  0.0 71.6 jit_solution(9468196977668591935)
XLA Ops:
  0.6 70.1 %shard_map.94 = (bf16[1,256,384]{2,1,0:T(8,128)(2,1)S(1)}, bf16[1,256,384]{2,1,0:T(8,128)(2,1)S(1)}, bf16[1,96,1024]{2,1,0:T(8,128)(2,1)S(1)}) custom-call(bf16[128,1024]{1,0:T(8,128)(2,1)} %tok.1, bf16[128,1024]{1,0:T(8,128)(2,1)} %cot.1, s32[3,128]{1,0:T(4,128)} %bitcast.2, f32[3,128]{1,0:T(4,128)} %bitcast.3, bf16[1,1024,384]{2,1,0:T(8,128)(2,1)} %wg_in.1, ...), custom_call_target="tpu_custom_call" | custom-call | tf_op jit(solution)/shard_map/pallas_call | solution.py:426
  70.7 0.8 %shard_map.95 = (bf16[1,256,384]{2,1,0:T(8,128)(2,1)}, bf16[1,256,384]{2,1,0:T(8,128)(2,1)}, bf16[1,96,1024]{2,1,0:T(8,128)(2,1)}) custom-call(bf16[1,256,384]{2,1,0:T(8,128)(2,1)S(1)} %get-tuple-element.6.refs_0_, bf16[1,256,384]{2,1,0:T(8,128)(2,1)S(1)} %get-tuple-element.7.refs_1_, bf16[1,96,1024]{2,1,0:T(8,128)(2,1)S(1)} %get-tuple-element.8.refs_2_), custom_call_target="tpu_custom_call" | custom-call | tf_op jit(solution)/shard_map/pallas_call | solution.py:375

commit v5 on v4

--- a/solution.py
+++ b/solution.py
@@ -10,7 +10,7 @@
 
 MESH = pl.DeviceIdType.MESH
 CORES = 2
-QUARTERS = 4
+QUARTERS = 2
 
 
 def kernel(

time: 71.8 us -> 67.7 us (0.943)
  Pallas kernels: 70.9 us -> 66.9 us
    pallas_call x1, Pallas kernels: 70.1 us -> 66.1 us  [step(): pl.pallas_call(functools.partial(kernel, n_e, n_a, n_b), out_shape=(jax.S...]
where the time goes in v5:
time: 67.7 us; the launch traced here: 67.6 us
  Pallas kernels  66.9 us (99%)
    pallas_call x1, Pallas kernels, step(): pl.pallas_call(functools.partial(kernel, n_e, n_a, n_b), out_shape=(jax.S...  66.1 us

profile of v5, /device:TPU:0, one launch (start us, length us, event | category | flops | bytes accessed | tf_op | source)
XLA Modules:
  0.0 67.6 jit_solution(16308971516371979020)
XLA Ops:
  0.6 66.1 %shard_map.94 = (bf16[1,256,384]{2,1,0:T(8,128)(2,1)S(1)}, bf16[1,256,384]{2,1,0:T(8,128)(2,1)S(1)}, bf16[1,96,1024]{2,1,0:T(8,128)(2,1)S(1)}) custom-call(bf16[128,1024]{1,0:T(8,128)(2,1)} %tok.1, bf16[128,1024]{1,0:T(8,128)(2,1)} %cot.1, s32[3,128]{1,0:T(4,128)} %bitcast.2, f32[3,128]{1,0:T(4,128)} %bitcast.3, bf16[1,1024,384]{2,1,0:T(8,128)(2,1)} %wg_in.1, ...), custom_call_target="tpu_custom_call" | custom-call | tf_op jit(solution)/shard_map/pallas_call | solution.py:426
  66.7 0.8 %shard_map.95 = (bf16[1,256,384]{2,1,0:T(8,128)(2,1)}, bf16[1,256,384]{2,1,0:T(8,128)(2,1)}, bf16[1,96,1024]{2,1,0:T(8,128)(2,1)}) custom-call(bf16[1,256,384]{2,1,0:T(8,128)(2,1)S(1)} %get-tuple-element.6.refs_0_, bf16[1,256,384]{2,1,0:T(8,128)(2,1)S(1)} %get-tuple-element.7.refs_1_, bf16[1,96,1024]{2,1,0:T(8,128)(2,1)S(1)} %get-tuple-element.8.refs_2_), custom_call_target="tpu_custom_call" | custom-call | tf_op jit(solution)/shard_map/pallas_call | solution.py:375
